TPU v7x, 32 devices: a whole 2x2x4 slice. The times are simulated.
32 devices in a mesh: fsdp: 2 (over x), context: 4 (over y, core), tensor: 4 (over z).
Axes of the slice: x: 2, y: 2, z: 4, core: 2. Of those that a mesh axis runs over, the one named last changes fastest.
Arguments:
- tokens: bfloat16 [2, 2048, 1024], P('fsdp', 'context'), may hold values from -6 to 6
- cotangent: bfloat16 [2, 2048, 1024], P('fsdp', 'context'), may hold values from -6 to 6
- lengths: int32 [2, 4], P('fsdp'), may hold values from 1 to 1024, 2048 in all within a row
- w_in: bfloat16 [3, 1024, 1024], P(None, 'fsdp', 'tensor'), may hold values from -0.1875 to 0.1875
- w_out: bfloat16 [1024, 1024], P('tensor', 'fsdp'), may hold values from -0.1875 to 0.1875
- w_gate_up: bfloat16 [2, 1024, 4608], P(None, 'fsdp', 'tensor'), may hold values from -0.1875 to 0.1875
- w_down: bfloat16 [4608, 1024], P('tensor', 'fsdp'), may hold values from -0.1875 to 0.1875
- norm_gains: bfloat16 [2, 1024], P(None, 'fsdp'), may hold values from 0.5 to 1.5
- conv_kernel: bfloat16 [3, 1024], P(None, 'tensor'), may hold values from -3 to 3
Outputs:
- block_out: float32 [2, 2048, 1024], P('fsdp', 'context')
- grad_tokens: float32 [2, 2048, 1024], P('fsdp', 'context')
- grad_w_in: float32 [3, 1024, 1024], P(None, 'fsdp', 'tensor')
- grad_w_out: float32 [1024, 1024], P('tensor', 'fsdp')
- grad_w_gate_up: float32 [2, 1024, 4608], P(None, 'fsdp', 'tensor')
- grad_w_down: float32 [4608, 1024], P('tensor', 'fsdp')
- grad_norm_gains: float32 [2, 1024], P(None, 'fsdp')
- grad_conv_kernel: float32 [3, 1024], P(None, 'tensor')
Inputs may be any that keep to these rules, and one draw needn't show every extreme that they name: `lengths`: each row of 2048 tokens is a pack of 4 whole documents, in order; some document of every row has 1024 tokens.
All inputs are finite; a program needn't handle non-finite values.
Results may differ from a plain program's by a relative error of at most 0.0088.
Values may be sent and summed in bfloat16 or wider, within the bound.
No kernel may reach another device: no remote copies, remote signals or barrier semaphores. Data moves between devices by JAX's collectives and lax.ppermute only.
A program may use at most 128 MiB of HBM per device.

v0:
```python
import jax
import jax.numpy as jnp
from jax import lax
from jax.sharding import PartitionSpec as P

norm_eps = 1e-05


def shifted(block, axis, distance):
    devices = range(lax.axis_size(axis))
    route = [(i - distance, i) for i in devices if i - distance in devices]
    return lax.ppermute(block, axis, route)


def matmul_plain(matrix_one, matrix_two):
    return jnp.dot(matrix_one, matrix_two, preferred_element_type=jnp.float32)


def matmul_right(matrix_one, matrix_two):
    return lax.dot_general(
        matrix_one, matrix_two, (((1,), (1,)), ((), ())), preferred_element_type=jnp.float32
    )


def matmul_left(matrix_one, matrix_two):
    return lax.dot_general(
        matrix_one, matrix_two, (((0,), (0,)), ((), ())), preferred_element_type=jnp.float32
    )


def norm_forward(values):
    inv_root = lax.rsqrt(jnp.mean(values * values, axis=-1, keepdims=True) + norm_eps)
    return (values * inv_root, inv_root)


def norm_backward(normed, inv_root, gain_row, grad_out):
    grad_normed = grad_out * gain_row
    inner_mean = jnp.mean(grad_normed * normed, axis=-1, keepdims=True)
    return (inv_root * (grad_normed - normed * inner_mean), jnp.sum(grad_out * normed, axis=0))


def keep_masks(position, lengths_row):
    starts = jnp.cumsum(lengths_row) - lengths_row
    doc_start = jnp.max(jnp.where(starts[None, :] <= position[:, None], starts[None, :], 0), axis=1)
    keep_one = (position - 1 >= doc_start).astype(jnp.float32)[:, None]
    keep_two = (position - 2 >= doc_start).astype(jnp.float32)[:, None]
    return (keep_one, keep_two)


def local(tokens, cotangent, lengths, w_in, w_out, w_gate_up, w_down, norm_gains, conv_kernel):
    block_rows = tokens.shape[1]
    position = lax.axis_index("context") * block_rows + jnp.arange(block_rows + 2, dtype=jnp.int32)
    keep_one_ext, keep_two_ext = keep_masks(position, lengths[0])
    keep_one = keep_one_ext[:block_rows]
    keep_two = keep_two_ext[:block_rows]
    full_in, full_out, full_gate_up, full_down, full_gains = (
        lax.all_gather(w_in, "fsdp", axis=1, tiled=True),
        lax.all_gather(w_out, "fsdp", axis=1, tiled=True),
        lax.all_gather(w_gate_up, "fsdp", axis=1, tiled=True),
        lax.all_gather(w_down, "fsdp", axis=1, tiled=True),
        lax.all_gather(norm_gains, "fsdp", axis=1, tiled=True),
    )
    inputs = tokens[0].astype(jnp.float32)
    gain_first = full_gains[0].astype(jnp.float32)
    gain_second = full_gains[1].astype(jnp.float32)
    kernel_taps = conv_kernel.astype(jnp.float32)
    normed_one, root_one = norm_forward(inputs)
    hidden_one = (normed_one * gain_first).astype(jnp.bfloat16)
    b_part = matmul_plain(hidden_one, full_in[0])
    c_part = matmul_plain(hidden_one, full_in[1])
    x_part = matmul_plain(hidden_one, full_in[2])
    mixed = b_part * x_part
    rim_rows = shifted(mixed[-2:], "context", 1)
    extended = jnp.concatenate([rim_rows, mixed], axis=0)
    back_one = extended[1:-1] * keep_one
    back_two = extended[:-2] * keep_two
    conv_value = kernel_taps[2] * mixed + kernel_taps[1] * back_one + kernel_taps[0] * back_two
    gated = (c_part * conv_value).astype(jnp.bfloat16)
    first_sum = inputs + lax.psum(matmul_plain(gated, full_out), "tensor")
    normed_two, root_two = norm_forward(first_sum)
    hidden_two = (normed_two * gain_second).astype(jnp.bfloat16)
    gate_value = matmul_plain(hidden_two, full_gate_up[0])
    up_value = matmul_plain(hidden_two, full_gate_up[1])
    sigmoid_gate = jax.nn.sigmoid(gate_value)
    silu_gate = gate_value * sigmoid_gate
    act_value = (silu_gate * up_value).astype(jnp.bfloat16)
    output_rows = first_sum + lax.psum(matmul_plain(act_value, full_down), "tensor")
    full_in, full_out, full_gate_up, full_down, full_gains = (
        lax.all_gather(w_in, "fsdp", axis=1, tiled=True),
        lax.all_gather(w_out, "fsdp", axis=1, tiled=True),
        lax.all_gather(w_gate_up, "fsdp", axis=1, tiled=True),
        lax.all_gather(w_down, "fsdp", axis=1, tiled=True),
        lax.all_gather(norm_gains, "fsdp", axis=1, tiled=True),
    )
    cot_rows = cotangent[0]
    grad_act = matmul_right(cot_rows, full_down)
    grad_gate = (
        grad_act * up_value * sigmoid_gate * (1.0 + gate_value * (1.0 - sigmoid_gate))
    ).astype(jnp.bfloat16)
    grad_up = (grad_act * silu_gate).astype(jnp.bfloat16)
    grad_h2 = lax.psum(
        matmul_right(grad_gate, full_gate_up[0]) + matmul_right(grad_up, full_gate_up[1]), "tensor"
    )
    back_second, grad_gain_two = norm_backward(normed_two, root_two, gain_second, grad_h2)
    grad_first = cot_rows.astype(jnp.float32) + back_second
    grad_first_b = grad_first.astype(jnp.bfloat16)
    grad_gated = matmul_right(grad_first_b, full_out)
    grad_conv = grad_gated * c_part
    next_rows = shifted(grad_conv[:2], "context", -1)
    ahead = jnp.concatenate([grad_conv, next_rows], axis=0)
    ahead_one = ahead[1 : block_rows + 1] * keep_one_ext[1 : block_rows + 1]
    ahead_two = ahead[2:] * keep_two_ext[2:]
    grad_mixed = (
        kernel_taps[2] * grad_conv + kernel_taps[1] * ahead_one + kernel_taps[0] * ahead_two
    )
    grad_kernel = jnp.stack(
        [
            jnp.sum(grad_conv * back_two, axis=0),
            jnp.sum(grad_conv * back_one, axis=0),
            jnp.sum(grad_conv * mixed, axis=0),
        ]
    )
    grad_b = (grad_mixed * x_part).astype(jnp.bfloat16)
    grad_c = (grad_gated * conv_value).astype(jnp.bfloat16)
    grad_x = (grad_mixed * b_part).astype(jnp.bfloat16)
    local_h1 = (
        matmul_right(grad_b, full_in[0])
        + matmul_right(grad_c, full_in[1])
        + matmul_right(grad_x, full_in[2])
    )
    grad_h1 = lax.psum(local_h1, "tensor")
    back_first, grad_gain_one = norm_backward(normed_one, root_one, gain_first, grad_h1)
    grad_inputs = grad_first + back_first
    term_in = jnp.stack(
        [
            matmul_left(hidden_one, grad_b),
            matmul_left(hidden_one, grad_c),
            matmul_left(hidden_one, grad_x),
        ]
    )
    term_out = matmul_left(gated, grad_first_b)
    term_gate_up = jnp.stack([matmul_left(hidden_two, grad_gate), matmul_left(hidden_two, grad_up)])
    term_down = matmul_left(act_value, cot_rows)
    term_gains = jnp.stack([grad_gain_one, grad_gain_two])
    pieces = (
        lax.psum_scatter(term_in, "fsdp", scatter_dimension=1, tiled=True),
        lax.psum_scatter(term_out, "fsdp", scatter_dimension=1, tiled=True),
        lax.psum_scatter(term_gate_up, "fsdp", scatter_dimension=1, tiled=True),
        lax.psum_scatter(term_down, "fsdp", scatter_dimension=1, tiled=True),
        lax.psum_scatter(term_gains, "fsdp", scatter_dimension=1, tiled=True),
    )
    reduced = lax.psum((pieces[0], pieces[1], pieces[2], pieces[3], pieces[4]), "context")
    kernel_total = lax.psum(grad_kernel, ("fsdp", "context"))
    return (
        output_rows[None],
        grad_inputs[None],
        reduced[0],
        reduced[1],
        reduced[2],
        reduced[3],
        reduced[4],
        kernel_total,
    )


def solution(mesh):
    placed = (
        P("fsdp", "context", None),
        P("fsdp", "context", None),
        P("fsdp", None),
        P(None, "fsdp", "tensor"),
        P("tensor", "fsdp"),
        P(None, "fsdp", "tensor"),
        P("tensor", "fsdp"),
        P(None, "fsdp"),
        P(None, "tensor"),
    )
    return jax.shard_map(
        local,
        mesh=mesh,
        in_specs=placed,
        out_specs=(
            P("fsdp", "context", None),
            P("fsdp", "context", None),
            P(None, "fsdp", "tensor"),
            P("tensor", "fsdp"),
            P(None, "fsdp", "tensor"),
            P("tensor", "fsdp"),
            P(None, "fsdp"),
            P(None, "tensor"),
        ),
        check_vma=False,
    )
```

profile of v0, /device:TPU:0, one launch (start us, length us, event | category | flops | bytes accessed | tf_op | source)
XLA Modules:
  0.0 958.6 jit_solution(321070914398784171)
XLA Ops:
  9.4 5.5 all_gather.19
  17.5 21.9 %all-gather.4.cloned.1.call-done = bf16[3,1024,256]{2,1,0:T(8,128)(2,1)} async-done(((bf16[3,512,256]{2,1,0:T(8,128)(2,1)}), bf16[3,1024,256]{2,1,0:T(8,128)(2,1)}) %all-gather.4.cloned.1.call-update) | async-done | bytes 1572880 | tf_op jit(solution)/shard_map/all_gather | solution.py:57
  44.4 8.9 all_gather.21
  58.7 84.5 %all-reduce.7.cloned.1.call-done = f32[512,1024]{1,0:T(8,128)} async-done(((f32[512,1024]{1,0:T(8,128)}), f32[512,1024]{1,0:T(8,128)}) %all-reduce.7.cloned.1.call-update) | async-done | bytes 2097168 | tf_op jit(solution)/shard_map/psum | solution.py:79
  146.4 60.0 %all-gather.6.cloned.1.call-done = bf16[2,1024,1152]{2,1,0:T(8,128)(2,1)} async-done(((bf16[2,512,1152]{2,1,0:T(8,128)(2,1)}), bf16[2,1024,1152]{2,1,0:T(8,128)(2,1)}) %all-gather.6.cloned.1.call-update) | async-done | bytes 4718608 | tf_op jit(solution)/shard_map/all_gather | solution.py:59
  206.4 5.1 fusion.19
  214.4 29.5 %all-gather.8.cloned.1.call-done = bf16[1152,1024]{1,0:T(8,128)(2,1)} async-done(((bf16[1152,512]{1,0:T(8,128)(2,1)}), bf16[1152,1024]{1,0:T(8,128)(2,1)}) %all-gather.8.cloned.1.call-update) | async-done | bytes 2359312 | tf_op jit(solution)/shard_map/all_gather | solution.py:60
  243.9 6.7 multiply_convert_fusion
  250.6 4.1 fusion.18
  254.6 4.5 fusion.22
  259.4 4.9 fusion.62
  264.3 81.2 %all-reduce.9.cloned.1.call-done = f32[512,1024]{1,0:T(8,128)} async-done(((f32[512,1024]{1,0:T(8,128)}), f32[512,1024]{1,0:T(8,128)}) %all-reduce.9.cloned.1.call-update) | async-done | bytes 2097168 | tf_op jit(solution)/shard_map/psum | solution.py:101
  366.6 5.2 fusion.24
  376.7 4.3 pad_maximum_fusion
  381.3 131.5 %all-reduce.11.cloned.1.call-done = (f32[512,1024]{1,0:T(8,128)}, f32[512,1024]{1,0:T(8,128)}) async-done(((f32[512,1024]{1,0:T(8,128)}, f32[512,1024]{1,0:T(8,128)}), (f32[512,1024]{1,0:T(8,128)}, f32[512,1024]{1,0:T(8,128)})) %all-reduce.11.cloned.1.call-update) | async-done | bytes 4194320 | tf_op jit(solution)/shard_map/psum | solution.py:87
  516.2 18.3 %reduce-scatter.10.cloned.1.call-done = f32[256,512]{1,0:T(8,128)} async-done(((f32[256,1024]{1,0:T(8,128)}), f32[256,512]{1,0:T(8,128)}) %reduce-scatter.10.cloned.1.call-update) | async-done | bytes 524304 | tf_op jit(solution)/shard_map/reduce_scatter | solution.py:147
  534.4 45.7 %reduce-scatter.8.cloned.1.call-done = f32[3,512,256]{2,1,0:T(8,128)} async-done(((f32[3,1024,256]{2,1,0:T(8,128)}), f32[3,512,256]{2,1,0:T(8,128)}) %reduce-scatter.8.cloned.1.call-update) | async-done | bytes 1572880 | tf_op jit(solution)/shard_map/reduce_scatter | solution.py:146
  580.1 63.0 %reduce-scatter.14.cloned.1.call-done = f32[1152,512]{1,0:T(8,128)} async-done(((f32[1152,1024]{1,0:T(8,128)}), f32[1152,512]{1,0:T(8,128)}) %reduce-scatter.14.cloned.1.call-update) | async-done | bytes 2359312 | tf_op jit(solution)/shard_map/reduce_scatter | solution.py:149
  643.1 112.8 %reduce-scatter.12.cloned.1.call-done = f32[2,512,1152]{2,1,0:T(8,128)} async-done(((f32[2,1024,1152]{2,1,0:T(8,128)}), f32[2,512,1152]{2,1,0:T(8,128)}) %reduce-scatter.12.cloned.1.call-update) | async-done | bytes 4718608 | tf_op jit(solution)/shard_map/reduce_scatter | solution.py:148
  756.0 13.1 %psum.79 = f32[3,256]{1,0:T(4,128)} all-reduce(f32[3,256]{1,0:T(4,128)S(1)} %pad_maximum_fusion.5), channel_id=1, replica_groups=mesh['fsdp'=2,'context'=4,'tensor'=4] {'fsdp','context'}, use_global_device_ids=true, to_apply=%region_25.26 | all-reduce | flops 768 | bytes 6144 | tf_op jit(solution)/shard_map/psum | solution.py:153
  769.1 3.6 add_bitcast_fusion
  775.8 6.3 psum.78
  782.1 159.7 %all-reduce.13.cloned.1.call-done = (f32[3,512,256]{2,1,0:T(8,128)}, f32[256,512]{1,0:T(8,128)}, f32[2,512,1152]{2,1,0:T(8,128)}, f32[1152,512]{1,0:T(8,128)}) async-done(((f32[3,512,256]{2,1,0:T(8,128)}, f32[256,512]{1,0:T(8,128)}, f32[2,512,1152]{2,1,0:T(8,128)}, f32[1152,512]{1,0:T(8,128)}), (f32[3,512,256]{2,1,0:T(8,128)}, f32[256,512]{1,0:T(8,128)}, f32[2,512,1152]{2,1,0:T(8,128)}, ...) | async-done | bytes 9175056 | tf_op jit(solution)/shard_map/psum | solution.py:152
  945.3 5.0 copy.29
  (136 shorter events, 58.8 us)
Async XLA Ops:
  7.2 32.3 %all-gather.4.cloned.1.call-start = ((), (), s32[]{:S(2)}) async-start(), calls=%async_computation.5 | async-start | bytes 2359296 | tf_op jit(solution)/shard_map/all_gather | solution.py:57
  7.9 135.3 %all-reduce.7.cloned.1.call-start = ((), (), s32[]{:S(2)}) async-start(), calls=%async_computation.6 | async-start | bytes 4194304 | tf_op jit(solution)/shard_map/psum | solution.py:79
  15.0 26.4 %copy-start.2 = (bf16[1,512,1024]{2,1,0:T(8,128)(2,1)S(1)}, bf16[1,512,1024]{2,1,0:T(8,128)(2,1)}, u32[]{:S(2)}) copy-start(bf16[1,512,1024]{2,1,0:T(8,128)(2,1)} %param.9) | copy-start | bytes 3145732
  42.8 12.1 %copy-start.20 = (f32[512,256]{1,0:T(8,128)}, f32[512,256]{1,0:T(8,128)S(1)}, u32[]{:S(2)}) copy-start(f32[512,256]{1,0:T(8,128)S(1)} %get-tuple-element.43) | copy-start | bytes 1572868
  42.8 10.5 %collective-permute-start = (f32[2,256]{1,0:T(2,128)S(1)}, f32[2,256]{1,0:T(2,128)S(1)}, u32[]{:S(2)}, u32[]{:S(2)}) collective-permute-start(f32[2,256]{1,0:T(2,128)S(1)} %slice.98), channel_id=1, source_target_pairs={{0,4},{4,8},{8,12},{1,5},{5,9},{9,13},{2,6},{6,10},{10,14},{3,7},{... | collective-permute-start | bytes 6152 | tf_op jit(solution)/shard_map/ppermute | solution.py:12
  57.3 149.1 %all-gather.6.cloned.1.call-start = ((), (), s32[]{:S(2)}) async-start(), calls=%async_computation.7 | async-start | bytes 7077888 | tf_op jit(solution)/shard_map/all_gather | solution.py:59
  58.1 185.8 %all-gather.8.cloned.1.call-start = ((), (), s32[]{:S(2)}) async-start(), calls=%async_computation.8 | async-start | bytes 3538944 | tf_op jit(solution)/shard_map/all_gather | solution.py:60
  58.7 286.9 %all-reduce.9.cloned.1.call-start = ((), (), s32[]{:S(2)}) async-start(), calls=%async_computation.9 | async-start | bytes 4194304 | tf_op jit(solution)/shard_map/psum | solution.py:101
  206.4 5.1 copy-start.3
  206.4 5.1 copy-start.29
  250.5 4.1 copy-start.13
  250.5 4.1 copy-start.15
  259.2 253.6 %all-reduce.11.cloned.1.call-start = ((), (), s32[]{:S(2)}) async-start(), calls=%async_computation.15 | async-start | bytes 8388608 | tf_op jit(solution)/shard_map/psum | solution.py:87
  351.5 3.5 copy-start.19
  351.5 3.2 collective-permute-start.1
  358.1 176.3 %reduce-scatter.10.cloned.1.call-start = ((), (), s32[]{:S(2)}) async-start(), calls=%async_computation.11 | async-start | bytes 1572864 | tf_op jit(solution)/shard_map/reduce_scatter | solution.py:147
  361.4 218.7 %reduce-scatter.8.cloned.1.call-start = ((), (), s32[]{:S(2)}) async-start(), calls=%async_computation.10 | async-start | bytes 4718592 | tf_op jit(solution)/shard_map/reduce_scatter | solution.py:146
  366.5 276.6 %reduce-scatter.14.cloned.1.call-start = ((), (), s32[]{:S(2)}) async-start(), calls=%async_computation.13 | async-start | bytes 7077888 | tf_op jit(solution)/shard_map/reduce_scatter | solution.py:149
  371.8 384.2 %reduce-scatter.12.cloned.1.call-start = ((), (), s32[]{:S(2)}) async-start(), calls=%async_computation.12 | async-start | bytes 14155776 | tf_op jit(solution)/shard_map/reduce_scatter | solution.py:148
  381.0 393.7 %reduce-scatter.16.cloned.1.call-start = ((), (), s32[]{:S(2)}) async-start(), calls=%async_computation.14 | async-start | bytes 786432
  516.1 425.7 %all-reduce.13.cloned.1.call-start = ((), (), s32[]{:S(2)}) async-start(), calls=%async_computation.16 | async-start | bytes 18350080 | tf_op jit(solution)/shard_map/psum | solution.py:152
  769.1 3.6 copy-start.1
  769.1 3.6 copy-start.6
  945.3 5.0 copy-start.10
  (20 other events, 42.0 us)
Sparse Core Ops, SparseCore 0:
  9.5 29.8 all-gather.3
  57.5 85.6 all-reduce.6
  144.7 61.6 all-gather.5
  207.8 36.0 all-gather.7
  259.3 86.1 all-reduce.8
  358.2 154.5 all-reduce.10
  515.0 19.3 reduce-scatter.9
  536.7 43.3 reduce-scatter.7
  583.0 60.0 reduce-scatter.13
  645.3 110.6 reduce-scatter.11
  758.8 14.6 reduce-scatter.15
  776.1 165.6 all-reduce.12
where the time goes:
time: 959 us
  waiting for transfers between devices  811 us (85%)
  matrix products  54 us (6%)
  blocking collectives  33.8 us (4%)
  other arithmetic  23.9 us (2%)
  local copies, waits for them, and re-layouts  17 us (2%)
  between operations  14.6 us (2%)
    psum x1, waiting for transfers between devices, local(): lax.psum((pieces[0], pieces[1], pieces[2], pieces[3], pieces[4]), 'context')  160 us
    psum x1, waiting for transfers between devices, local(): lax.psum(matmul_plain(act_value, full_down), 'tensor')  131 us
    reduce_scatter x1, waiting for transfers between devices, local(): lax.psum_scatter(term_gate_up, 'fsdp', scatter_dimension=1, tiled=True)  113 us
    psum x1, waiting for transfers between devices, local(): first_sum = inputs + lax.psum(matmul_plain(gated, full_out), 'tensor')  84.5 us
    psum x1, waiting for transfers between devices, local(): lax.psum(matmul_right(grad_gate, full_gate_up[0]) + matmul_right(grad_up,...  81.2 us
    reduce_scatter x1, waiting for transfers between devices, local(): lax.psum_scatter(term_down, 'fsdp', scatter_dimension=1, tiled=True)  63 us
    all_gather x1, waiting for transfers between devices, local(): lax.all_gather(w_gate_up, 'fsdp', axis=1, tiled=True)  60 us
    reduce_scatter x1, waiting for transfers between devices, local(): lax.psum_scatter(term_in, 'fsdp', scatter_dimension=1, tiled=True)  45.7 us
  transfers between devices with their start and end apart: 14, of which 12 were waited for; matrix products, arithmetic and copies ran while one was open for 5% of the time, Pallas kernels for 0%

commit v1 on v0

--- a/solution.py
+++ b/solution.py
@@ -4,6 +4,27 @@
 from jax.sharding import PartitionSpec as P
 
 norm_eps = 1e-05
+
+
+def in_order(blocks, dim):
+    shape = list(blocks.shape[1:])
+    shape[dim] *= blocks.shape[0]
+    return jnp.moveaxis(blocks, 0, dim).reshape(shape)
+
+
+def collected_by_bits(value, axis):
+    length, here = (lax.axis_size(axis), lax.axis_index(axis))
+    blocks, bit = (value[None], 1)
+    while bit < length:
+        other = lax.ppermute(blocks, axis, [(i, i ^ bit) for i in range(length)])
+        low = here & bit == 0
+        blocks = jnp.concatenate([jnp.where(low, blocks, other), jnp.where(low, other, blocks)])
+        bit *= 2
+    return blocks
+
+
+def collect(x, axis, dim):
+    return in_order(collected_by_bits(x, axis), dim)
 
 
 def shifted(block, axis, distance):
@@ -56,7 +77,7 @@
     full_in, full_out, full_gate_up, full_down, full_gains = (
         lax.all_gather(w_in, "fsdp", axis=1, tiled=True),
         lax.all_gather(w_out, "fsdp", axis=1, tiled=True),
-        lax.all_gather(w_gate_up, "fsdp", axis=1, tiled=True),
+        collect(w_gate_up, "fsdp", 1),
         lax.all_gather(w_down, "fsdp", axis=1, tiled=True),
         lax.all_gather(norm_gains, "fsdp", axis=1, tiled=True),
     )

time: 959 us -> 955 us (level)
    psum x1, waiting for transfers between devices: 84.5 us -> 51.3 us  [local(): first_sum = inputs + lax.psum(matmul_plain(gated, full_out), 'tensor')]
    ppermute x0 -> x1, waiting for transfers between devices: none -> 28.8 us  [collected_by_bits(): other = lax.ppermute(blocks, axis, [(i, i ^ bit) for i in range(length)])]
  transfers between devices with their start and end apart: 14 -> 15, of which waited for: 12 -> 13; matrix products, arithmetic and copies ran while one was open for 5% -> 7% of each run, Pallas kernels for 0% -> 0%
where the time goes in v1:
time: 955 us
  waiting for transfers between devices  807 us (85%)
  matrix products  47.5 us (5%)
  blocking collectives  35 us (4%)
  other arithmetic  24.1 us (3%)
  local copies, waits for them, and re-layouts  21.5 us (2%)
  between operations  14.7 us (2%)
    psum x1, waiting for transfers between devices, local(): lax.psum((pieces[0], pieces[1], pieces[2], pieces[3], pieces[4]), 'context')  160 us
    psum x1, waiting for transfers between devices, local(): lax.psum(matmul_plain(act_value, full_down), 'tensor')  132 us
    reduce_scatter x1, waiting for transfers between devices, local(): lax.psum_scatter(term_gate_up, 'fsdp', scatter_dimension=1, tiled=True)  113 us
    psum x1, waiting for transfers between devices, local(): lax.psum(matmul_right(grad_gate, full_gate_up[0]) + matmul_right(grad_up,...  81.2 us
    reduce_scatter x1, waiting for transfers between devices, local(): lax.psum_scatter(term_down, 'fsdp', scatter_dimension=1, tiled=True)  63 us
    all_gather x1, waiting for transfers between devices, local(): lax.all_gather(w_gate_up, 'fsdp', axis=1, tiled=True)  52.5 us
    psum x1, waiting for transfers between devices, local(): first_sum = inputs + lax.psum(matmul_plain(gated, full_out), 'tensor')  51.3 us
    reduce_scatter x1, waiting for transfers between devices, local(): lax.psum_scatter(term_in, 'fsdp', scatter_dimension=1, tiled=True)  45.7 us
  transfers between devices with their start and end apart: 15, of which 13 were waited for; matrix products, arithmetic and copies ran while one was open for 7% of the time, Pallas kernels for 0%

profile of v1, /device:TPU:0, one launch (start us, length us, event | category | flops | bytes accessed | tf_op | source)
XLA Modules:
  0.0 954.8 jit_solution(4934432955511233261)
XLA Ops:
  10.5 5.3 all_gather.18
  16.0 23.4 %all-gather.4.cloned.1.call-done = bf16[3,1024,256]{2,1,0:T(8,128)(2,1)} async-done(((bf16[3,512,256]{2,1,0:T(8,128)(2,1)}), bf16[3,1024,256]{2,1,0:T(8,128)(2,1)}) %all-gather.4.cloned.1.call-update) | async-done | bytes 1572880 | tf_op jit(solution)/shard_map/all_gather | solution.py:78
  44.1 10.2 %all_gather.20 = bf16[256,1024]{1,0:T(8,128)(2,1)S(1)} all-gather(bf16[256,512]{1,0:T(8,128)(2,1)S(1)} %copy-done.31), channel_id=1, replica_groups=mesh['fsdp'=2,'context'=4,'tensor'=4] {'fsdp'}, dimensions={1}, use_global_device_ids=true | all-gather | bytes 786432 | tf_op jit(solution)/shard_map/all_gather | solution.py:79
  59.3 36.4 %all-gather.6.cloned.1.call-done = bf16[1152,1024]{1,0:T(8,128)(2,1)} async-done(((bf16[1152,512]{1,0:T(8,128)(2,1)}), bf16[1152,1024]{1,0:T(8,128)(2,1)}) %all-gather.6.cloned.1.call-update) | async-done | bytes 2359312 | tf_op jit(solution)/shard_map/all_gather | solution.py:81
  95.6 4.8 fusion.24
  100.4 28.8 %collective-permute-done.1 = bf16[1,2,512,1152]{3,2,1,0:T(8,128)(2,1)} collective-permute-done((bf16[1,2,512,1152]{3,2,1,0:T(8,128)(2,1)}, bf16[1,2,512,1152]{3,2,1,0:T(8,128)(2,1)}, u32[]{:S(2)}, u32[]{:S(2)}) %collective-permute-start.1) | collective-permute-done | bytes 2359328 | tf_op jit(solution)/shard_map/ppermute | solution.py:19
  134.4 51.3 %all-reduce.7.cloned.1.call-done = f32[512,1024]{1,0:T(8,128)} async-done(((f32[512,1024]{1,0:T(8,128)}), f32[512,1024]{1,0:T(8,128)}) %all-reduce.7.cloned.1.call-update) | async-done | bytes 2097168 | tf_op jit(solution)/shard_map/psum | solution.py:100
  192.1 4.2 multiply_convert_fusion.1
  196.3 52.5 %all-gather.8.cloned.1.call-done = bf16[2,1024,1152]{2,1,0:T(8,128)(2,1)} async-done(((bf16[2,512,1152]{2,1,0:T(8,128)(2,1)}), bf16[2,1024,1152]{2,1,0:T(8,128)(2,1)}) %all-gather.8.cloned.1.call-update) | async-done | bytes 4718608 | tf_op jit(solution)/shard_map/all_gather | solution.py:112
  248.8 3.7 fusion.7
  255.7 4.9 fusion.62
  260.6 81.2 %all-reduce.9.cloned.1.call-done = f32[512,1024]{1,0:T(8,128)} async-done(((f32[512,1024]{1,0:T(8,128)}), f32[512,1024]{1,0:T(8,128)}) %all-reduce.9.cloned.1.call-update) | async-done | bytes 2097168 | tf_op jit(solution)/shard_map/psum | solution.py:122
  362.7 5.2 fusion.22
  372.9 4.3 pad_maximum_fusion
  377.5 131.6 %all-reduce.11.cloned.1.call-done = (f32[512,1024]{1,0:T(8,128)}, f32[512,1024]{1,0:T(8,128)}) async-done(((f32[512,1024]{1,0:T(8,128)}, f32[512,1024]{1,0:T(8,128)}), (f32[512,1024]{1,0:T(8,128)}, f32[512,1024]{1,0:T(8,128)})) %all-reduce.11.cloned.1.call-update) | async-done | bytes 4194320 | tf_op jit(solution)/shard_map/psum | solution.py:108
  512.4 18.3 %reduce-scatter.10.cloned.1.call-done = f32[256,512]{1,0:T(8,128)} async-done(((f32[256,1024]{1,0:T(8,128)}), f32[256,512]{1,0:T(8,128)}) %reduce-scatter.10.cloned.1.call-update) | async-done | bytes 524304 | tf_op jit(solution)/shard_map/reduce_scatter | solution.py:168
  530.7 45.7 %reduce-scatter.8.cloned.1.call-done = f32[3,512,256]{2,1,0:T(8,128)} async-done(((f32[3,1024,256]{2,1,0:T(8,128)}), f32[3,512,256]{2,1,0:T(8,128)}) %reduce-scatter.8.cloned.1.call-update) | async-done | bytes 1572880 | tf_op jit(solution)/shard_map/reduce_scatter | solution.py:167
  576.4 63.0 %reduce-scatter.14.cloned.1.call-done = f32[1152,512]{1,0:T(8,128)} async-done(((f32[1152,1024]{1,0:T(8,128)}), f32[1152,512]{1,0:T(8,128)}) %reduce-scatter.14.cloned.1.call-update) | async-done | bytes 2359312 | tf_op jit(solution)/shard_map/reduce_scatter | solution.py:170
  639.4 112.8 %reduce-scatter.12.cloned.1.call-done = f32[2,512,1152]{2,1,0:T(8,128)} async-done(((f32[2,1024,1152]{2,1,0:T(8,128)}), f32[2,512,1152]{2,1,0:T(8,128)}) %reduce-scatter.12.cloned.1.call-update) | async-done | bytes 4718608 | tf_op jit(solution)/shard_map/reduce_scatter | solution.py:169
  752.2 13.1 %psum.79 = f32[3,256]{1,0:T(4,128)} all-reduce(f32[3,256]{1,0:T(4,128)S(1)} %pad_maximum_fusion.5), channel_id=1, replica_groups=mesh['fsdp'=2,'context'=4,'tensor'=4] {'fsdp','context'}, use_global_device_ids=true, to_apply=%region_25.26 | all-reduce | flops 768 | bytes 6144 | tf_op jit(solution)/shard_map/psum | solution.py:174
  765.4 3.6 add_bitcast_fusion
  772.0 6.3 psum.78
  778.3 159.7 %all-reduce.13.cloned.1.call-done = (f32[3,512,256]{2,1,0:T(8,128)}, f32[256,512]{1,0:T(8,128)}, f32[2,512,1152]{2,1,0:T(8,128)}, f32[1152,512]{1,0:T(8,128)}) async-done(((f32[3,512,256]{2,1,0:T(8,128)}, f32[256,512]{1,0:T(8,128)}, f32[2,512,1152]{2,1,0:T(8,128)}, f32[1152,512]{1,0:T(8,128)}), (f32[3,512,256]{2,1,0:T(8,128)}, f32[256,512]{1,0:T(8,128)}, f32[2,512,1152]{2,1,0:T(8,128)}, ...) | async-done | bytes 9175056 | tf_op jit(solution)/shard_map/psum | solution.py:173
  941.6 5.0 copy.29
  (153 shorter events, 64.9 us)
Async XLA Ops:
  7.2 8.7 copy-start.32
  7.2 32.3 %all-gather.4.cloned.1.call-start = ((), (), s32[]{:S(2)}) async-start(), calls=%async_computation.5 | async-start | bytes 2359296 | tf_op jit(solution)/shard_map/all_gather | solution.py:78
  7.9 87.7 %all-gather.6.cloned.1.call-start = ((), (), s32[]{:S(2)}) async-start(), calls=%async_computation.7 | async-start | bytes 3538944 | tf_op jit(solution)/shard_map/all_gather | solution.py:81
  8.7 177.0 %all-reduce.7.cloned.1.call-start = ((), (), s32[]{:S(2)}) async-start(), calls=%async_computation.6 | async-start | bytes 4194304 | tf_op jit(solution)/shard_map/psum | solution.py:100
  42.5 13.4 %copy-start.23 = (f32[512,256]{1,0:T(8,128)}, f32[512,256]{1,0:T(8,128)S(1)}, u32[]{:S(2)}) copy-start(f32[512,256]{1,0:T(8,128)S(1)} %get-tuple-element.47) | copy-start | bytes 1572868
  42.5 11.8 %collective-permute-start = (f32[2,256]{1,0:T(2,128)S(1)}, f32[2,256]{1,0:T(2,128)S(1)}, u32[]{:S(2)}, u32[]{:S(2)}) collective-permute-start(f32[2,256]{1,0:T(2,128)S(1)} %slice.106), channel_id=1, source_target_pairs={{0,4},{4,8},{8,12},{1,5},{5,9},{9,13},{2,6},{6,10},{10,14},{3,7},{... | collective-permute-start | bytes 6152 | tf_op jit(solution)/shard_map/ppermute | solution.py:33
  58.4 37.3 %copy-start.10 = (bf16[1,512,1024]{2,1,0:T(8,128)(2,1)S(1)}, bf16[1,512,1024]{2,1,0:T(8,128)(2,1)}, u32[]{:S(2)}) copy-start(bf16[1,512,1024]{2,1,0:T(8,128)(2,1)} %param.10) | copy-start | bytes 3145732
  58.4 190.4 %all-gather.8.cloned.1.call-start = ((), (), s32[]{:S(2)}) async-start(), calls=%async_computation.8 | async-start | bytes 7077888 | tf_op jit(solution)/shard_map/all_gather | solution.py:112
  58.4 70.8 %collective-permute-start.1 = (bf16[1,2,512,1152]{3,2,1,0:T(8,128)(2,1)}, bf16[1,2,512,1152]{3,2,1,0:T(8,128)(2,1)}, u32[]{:S(2)}, u32[]{:S(2)}) collective-permute-start(bf16[1,2,512,1152]{3,2,1,0:T(8,128)(2,1)} %bitcast.134), channel_id=1, source_target_pairs={{0,16},{16,0},{1,17},{17,1},{2,18},{18,2},{3,19},{19,3},{4,20},{20... | collective-permute-start | bytes 7077896 | tf_op jit(solution)/shard_map/ppermute | solution.py:19
  59.2 282.5 %all-reduce.9.cloned.1.call-start = ((), (), s32[]{:S(2)}) async-start(), calls=%async_computation.9 | async-start | bytes 4194304 | tf_op jit(solution)/shard_map/psum | solution.py:122
  95.6 33.6 %copy-start.3 = (bf16[2,512,1152]{2,1,0:T(8,128)(2,1)S(1)}, bf16[2,512,1152]{2,1,0:T(8,128)(2,1)}, u32[]{:S(2)}) copy-start(bf16[2,512,1152]{2,1,0:T(8,128)(2,1)} %param.14) | copy-start | bytes 7077892
  248.8 3.7 copy-start.17
  248.8 3.8 copy-start.34
  255.5 253.6 %all-reduce.11.cloned.1.call-start = ((), (), s32[]{:S(2)}) async-start(), calls=%async_computation.15 | async-start | bytes 8388608 | tf_op jit(solution)/shard_map/psum | solution.py:108
  347.8 3.2 collective-permute-start.2
  354.4 176.3 %reduce-scatter.10.cloned.1.call-start = ((), (), s32[]{:S(2)}) async-start(), calls=%async_computation.11 | async-start | bytes 1572864 | tf_op jit(solution)/shard_map/reduce_scatter | solution.py:168
  357.6 218.8 %reduce-scatter.8.cloned.1.call-start = ((), (), s32[]{:S(2)}) async-start(), calls=%async_computation.10 | async-start | bytes 4718592 | tf_op jit(solution)/shard_map/reduce_scatter | solution.py:167
  362.7 276.7 %reduce-scatter.14.cloned.1.call-start = ((), (), s32[]{:S(2)}) async-start(), calls=%async_computation.13 | async-start | bytes 7077888 | tf_op jit(solution)/shard_map/reduce_scatter | solution.py:170
  367.9 384.3 %reduce-scatter.12.cloned.1.call-start = ((), (), s32[]{:S(2)}) async-start(), calls=%async_computation.12 | async-start | bytes 14155776 | tf_op jit(solution)/shard_map/reduce_scatter | solution.py:169
  377.2 393.7 %reduce-scatter.16.cloned.1.call-start = ((), (), s32[]{:S(2)}) async-start(), calls=%async_computation.14 | async-start | bytes 786432
  512.4 425.7 %all-reduce.13.cloned.1.call-start = ((), (), s32[]{:S(2)}) async-start(), calls=%async_computation.16 | async-start | bytes 18350080 | tf_op jit(solution)/shard_map/psum | solution.py:173
  765.4 3.6 copy-start.1
  765.4 3.6 copy-start.7
  941.6 5.0 copy-start.12
  (27 other events, 61.1 us)
Sparse Core Ops, SparseCore 0:
  9.5 29.8 all-gather.3
  41.0 54.5 all-gather.5
  98.6 87.0 all-reduce.6
  187.1 61.6 all-gather.7
  255.6 86.1 all-reduce.8
  354.5 154.5 all-reduce.10
  511.3 19.3 reduce-scatter.9
  532.9 43.3 reduce-scatter.7
  579.3 60.0 reduce-scatter.13
  641.5 110.6 reduce-scatter.11
  755.0 14.6 reduce-scatter.15
  772.4 165.6 all-reduce.12
